TPU v7x, 32 devices: a whole 2x2x4 slice. The times are simulated.
32 devices in a mesh: dp: 8 (over y, x, core), seq: 4 (over z).
Axes of the slice: x: 2, y: 2, z: 4, core: 2. Of those that a mesh axis runs over, the one named last changes fastest.
Arguments:
- queries: bfloat16 [4096, 4096], P(('dp', 'seq')), may hold values from -300 to 300
- key_proj: bfloat16 [4096, 512], P(('dp', 'seq')), may hold values from -4.5 to 4.5
- value_proj: bfloat16 [4096, 512], P(('dp', 'seq')), may hold values from -6 to 6
- seq_lengths: int32 [32], replicated, may hold values from 1 to 257, 4096 in all
Outputs:
- attended: bfloat16 [4096, 4096], P(('dp', 'seq'))
Inputs may be any that keep to these rules, and one draw needn't show every extreme that they name: `seq_lengths`: the sequences cover all 4096 tokens; the longest has exactly 257 tokens.
All inputs are finite; a program needn't handle non-finite values.
Results may differ from a plain program's by a relative error of at most 0.0036.
Values may be sent and summed in bfloat16 or wider, within the bound.
No kernel may reach another device: no remote copies, remote signals or barrier semaphores. Data moves between devices by JAX's collectives and lax.ppermute only.
A program may use at most 64 MiB of HBM per device.

v0:
```python
import math
import jax
import jax.numpy as jnp
from jax import lax
from jax.sharding import PartitionSpec as P

HD = 128
QH = 32
KVH = 4
score_scale = 0.08838834764831845
neg_fill = -1e30


def from_behind(block, axis, distance):
    devices = range(lax.axis_size(axis))
    route = [(i - distance, i) for i in devices if i - distance in devices]
    return lax.ppermute(block, axis, route)


def segment_starts(seq_lengths, positions):
    seq_ends = jnp.cumsum(seq_lengths)
    begins = seq_ends - seq_lengths
    covered = begins[None, :] <= positions[:, None]
    return jnp.max(jnp.where(covered, begins[None, :], 0), axis=1)


def attend(
    queries,
    own_keys,
    own_values,
    tail_keys,
    tail_values,
    query_pos,
    key_pos,
    tail_pos,
    query_start,
    tail_limit,
):
    row_count = queries.shape[0]
    heads_query = queries.shape[1]
    group_size = heads_query // own_keys.shape[1]
    tile_rows = math.gcd(row_count, 512)
    tail_count = tail_keys.shape[0]
    pieces = []
    for offset in range(0, row_count, tile_rows):
        query_tile = queries[offset : offset + tile_rows]
        pos_tile = query_pos[offset : offset + tile_rows]
        start_tile = query_start[offset : offset + tile_rows]
        key_count = offset + tile_rows
        keys_used = own_keys[:key_count]
        values_used = own_values[:key_count]
        pos_used = key_pos[:key_count]
        own_mask = (pos_used[None, :] <= pos_tile[:, None]) & (
            pos_used[None, :] >= start_tile[:, None]
        )
        use_tail = offset < tail_limit
        tail_mask = tail_pos[None, :] >= start_tile[:, None]
        reached = jnp.any(tail_mask)

        def one_head(head_index):
            shared_index = head_index // group_size
            query_head = lax.dynamic_index_in_dim(query_tile, head_index, 1, keepdims=False)
            key_head = lax.dynamic_index_in_dim(keys_used, shared_index, 1, keepdims=False)
            value_head = lax.dynamic_index_in_dim(values_used, shared_index, 1, keepdims=False)
            own_scores = (
                jnp.einsum("qd,kd->qk", query_head, key_head, preferred_element_type=jnp.float32)
                * score_scale
            )
            own_scores = jnp.where(own_mask, own_scores, neg_fill)
            row_max = jnp.max(own_scores, axis=1)
            if use_tail:
                tail_key = lax.dynamic_index_in_dim(tail_keys, shared_index, 1, keepdims=False)
                tail_value = lax.dynamic_index_in_dim(tail_values, shared_index, 1, keepdims=False)

                def tail_scores_fn():
                    raw = (
                        jnp.einsum(
                            "qd,kd->qk", query_head, tail_key, preferred_element_type=jnp.float32
                        )
                        * score_scale
                    )
                    return jnp.where(tail_mask, raw, neg_fill)

                def tail_empty():
                    return jnp.full((tile_rows, tail_count), neg_fill, jnp.float32)

                tail_scores = lax.cond(reached, tail_scores_fn, tail_empty)
                row_max = jnp.maximum(row_max, jnp.max(tail_scores, axis=1))
            own_weights = jnp.where(own_mask, jnp.exp(own_scores - row_max[:, None]), 0.0)
            row_sum = jnp.sum(own_weights, axis=1)
            weighted = jnp.dot(
                own_weights.astype(jnp.bfloat16), value_head, preferred_element_type=jnp.float32
            )
            if use_tail:
                tail_weights = jnp.where(tail_mask, jnp.exp(tail_scores - row_max[:, None]), 0.0)
                row_sum = row_sum + jnp.sum(tail_weights, axis=1)

                def tail_product():
                    return jnp.dot(
                        tail_weights.astype(jnp.bfloat16),
                        tail_value,
                        preferred_element_type=jnp.float32,
                    )

                def tail_zero():
                    return jnp.zeros((tile_rows, value_head.shape[1]), jnp.float32)

                weighted = weighted + lax.cond(reached, tail_product, tail_zero)
            return (weighted / row_sum[:, None]).astype(jnp.bfloat16)

        per_head = lax.map(one_head, jnp.arange(heads_query, dtype=jnp.int32))
        pieces.append(jnp.transpose(per_head, (1, 0, 2)))
    return jnp.concatenate(pieces, axis=0)


def body(queries, key_proj, value_proj, seq_lengths):
    tok_rows = queries.shape[0]
    members = lax.axis_size("seq")
    home_index = lax.axis_index("dp")
    block_rows = tok_rows * members
    reach_rows = block_rows // 2
    block_start = home_index * block_rows
    key_pos = block_start + jnp.arange(block_rows, dtype=jnp.int32)
    tail_pos = block_start - reach_rows + jnp.arange(reach_rows, dtype=jnp.int32)
    local_heads = QH // members
    copies = max(1, members // KVH)
    query_split = queries.reshape(tok_rows, members, local_heads * HD)
    key_split = key_proj.reshape(tok_rows, KVH, HD)
    value_split = value_proj.reshape(tok_rows, KVH, HD)
    if copies > 1:
        key_split = jnp.repeat(key_split, copies, axis=1)
        value_split = jnp.repeat(value_split, copies, axis=1)
    query_block, key_block, value_block = (
        lax.all_to_all(query_split, "seq", split_axis=1, concat_axis=0, tiled=True),
        lax.all_to_all(key_split, "seq", split_axis=1, concat_axis=0, tiled=True),
        lax.all_to_all(value_split, "seq", split_axis=1, concat_axis=0, tiled=True),
    )
    query_block = query_block.reshape(block_rows, local_heads, HD)
    tail_keys, tail_values = from_behind(
        (key_block[reach_rows:], value_block[reach_rows:]), "dp", 1
    )
    starts = segment_starts(seq_lengths, key_pos)
    mixed = attend(
        query_block,
        key_block,
        value_block,
        tail_keys,
        tail_values,
        key_pos,
        key_pos,
        tail_pos,
        starts,
        reach_rows,
    )
    mixed = mixed.reshape(block_rows, 1, local_heads * HD)
    returned = lax.all_to_all(mixed, "seq", split_axis=0, concat_axis=1, tiled=True)
    return returned.reshape(tok_rows, QH * HD)


def solution(mesh):
    return jax.shard_map(
        body,
        mesh=mesh,
        in_specs=(P(("dp", "seq"), None), P(("dp", "seq"), None), P(("dp", "seq"), None), P()),
        out_specs=P(("dp", "seq"), None),
        check_vma=False,
    )
```

profile of v0, /device:TPU:4, one launch (start us, length us, event | category | flops | bytes accessed | tf_op | source)
XLA Modules:
  0.0 136.4 jit_solution(15620430314450670122)
XLA Ops:
  0.0 1.7 %copy.50 = bf16[128,512]{0,1:T(8,128)(2,1)} copy(bf16[128,512]{1,0:T(8,128)(2,1)} %param.11) | data formatting | bytes 262144 | tf_op args[1]
  1.7 4.9 %all-to-all-start.1 = ((bf16[128,4,128]{0,2,1:T(8,128)(2,1)}), bf16[128,4,128]{0,2,1:T(8,128)(2,1)S(1)}, u32[]{:S(2)}, u32[]{:S(2)}) async-start(bf16[128,4,128]{0,2,1:T(8,128)(2,1)} %bitcast.5), calls=%async_computation.1 | async-start | bytes 262144 | tf_op jit(solution)/shard_map/all_to_all | solution.py:135
  6.5 1.7 %copy.54 = bf16[128,512]{0,1:T(8,128)(2,1)} copy(bf16[128,512]{1,0:T(8,128)(2,1)} %param.12) | data formatting | bytes 262144 | tf_op args[2]
  8.2 4.4 %all-to-all-done.1 = bf16[128,4,128]{0,2,1:T(8,128)(2,1)S(1)} async-done(((bf16[128,4,128]{0,2,1:T(8,128)(2,1)}), bf16[128,4,128]{0,2,1:T(8,128)(2,1)S(1)}, u32[]{:S(2)}, u32[]{:S(2)}) %all-to-all-start.1) | async-done | bytes 131104 | tf_op jit(solution)/shard_map/all_to_all | solution.py:135
  12.6 3.3 %all-to-all-start.2 = ((bf16[128,4,128]{0,2,1:T(8,128)(2,1)}), bf16[128,4,128]{0,2,1:T(8,128)(2,1)S(1)}, u32[]{:S(2)}, u32[]{:S(2)}) async-start(bf16[128,4,128]{0,2,1:T(8,128)(2,1)} %bitcast.12), calls=%async_computation.2 | async-start | bytes 262144 | tf_op jit(solution)/shard_map/all_to_all | solution.py:136
  16.0 2.3 %copy.70 = bf16[16,4,8,1024]{3,2,0,1:T(8,128)(2,1)} copy(bf16[16,4,8,1024]{3,2,1,0:T(8,128)(2,1)} %bitcast.80) | data formatting | bytes 2097152 | tf_op jit(solution)/shard_map/reshape | solution.py:127
  18.3 3.6 %all-to-all-done.2 = bf16[128,4,128]{0,2,1:T(8,128)(2,1)S(1)} async-done(((bf16[128,4,128]{0,2,1:T(8,128)(2,1)}), bf16[128,4,128]{0,2,1:T(8,128)(2,1)S(1)}, u32[]{:S(2)}, u32[]{:S(2)}) %all-to-all-start.2) | async-done | bytes 131104 | tf_op jit(solution)/shard_map/all_to_all | solution.py:136
  21.8 3.5 %all-to-all-start = ((bf16[128,4,1024]{2,0,1:T(8,128)(2,1)}), bf16[128,4,1024]{2,0,1:T(8,128)(2,1)S(1)}, u32[]{:S(2)}, u32[]{:S(2)}) async-start(bf16[128,4,1024]{2,0,1:T(8,128)(2,1)} %bitcast.58), calls=%async_computation | async-start | bytes 2097152 | tf_op jit(solution)/shard_map/all_to_all | solution.py:134
  25.9 1.9 %collective-permute-start = (bf16[256,1,128]{2,0,1:T(8,128)(2,1)S(1)}, bf16[256,1,128]{2,0,1:T(8,128)(2,1)S(1)}, u32[]{:S(2)}, u32[]{:S(2)}) collective-permute-start(bf16[256,1,128]{2,0,1:T(8,128)(2,1)S(1)} %bitcast.91), channel_id=1, source_target_pairs={{0,4},{4,8},{8,12},{12,16},{16,20},{20,24},{24,28},{1,5},{5,9},{9,... | collective-permute-start | bytes 196616 | tf_op jit(solution)/shard_map/ppermute | solution.py:17
  28.0 3.5 %collective-permute-start.1 = (bf16[256,1,128]{2,0,1:T(8,128)(2,1)S(1)}, bf16[256,1,128]{2,0,1:T(8,128)(2,1)S(1)}, u32[]{:S(2)}, u32[]{:S(2)}) collective-permute-start(bf16[256,1,128]{2,0,1:T(8,128)(2,1)S(1)} %bitcast.92), channel_id=1, source_target_pairs={{0,4},{4,8},{8,12},{12,16},{16,20},{20,24},{24,28},{1,5},{5,9},{9,... | collective-permute-start | bytes 196616 | tf_op jit(solution)/shard_map/ppermute | solution.py:17
  31.5 0.9 compare_reduce_fusion
  32.6 16.2 %all-to-all-done = bf16[128,4,1024]{2,0,1:T(8,128)(2,1)S(1)} async-done(((bf16[128,4,1024]{2,0,1:T(8,128)(2,1)}), bf16[128,4,1024]{2,0,1:T(8,128)(2,1)S(1)}, u32[]{:S(2)}, u32[]{:S(2)}) %all-to-all-start) | async-done | bytes 1048608 | tf_op jit(solution)/shard_map/all_to_all | solution.py:134
  49.2 51.4 %while.12 = (s32[]{:T(128)}, bf16[8,512,128]{1,2,0:T(8,128)(2,1)}, s32[8]{0:T(128)S(1)}, bf16[512,8,128]{2,0,1:T(8,128)(2,1)S(1)}, bf16[512,1,128]{2,0,1:T(8,128...) while((s32[]{:T(128)}, bf16[8,512,128]{1,2,0:T(8,128)(2,1)}, ...), condition=%wide.region_12.13_spmd.clone.clone, body=%wide.region_3.12_spmd.clone.clone.sunk | while | flops 207420416 | bytes 8435984 | solution.py:111
  52.4 0.7 conditional.8
  55.0 0.7 constant_dynamic-update-slice_fusion.2
  58.8 0.7 conditional.8
  61.4 0.7 constant_dynamic-update-slice_fusion.2
  65.2 0.7 conditional.8
  67.9 0.7 constant_dynamic-update-slice_fusion.2
  71.7 0.7 conditional.8
  74.3 0.7 constant_dynamic-update-slice_fusion.2
  78.1 0.7 conditional.8
  80.7 0.7 constant_dynamic-update-slice_fusion.2
  84.5 0.7 conditional.8
  87.1 0.7 constant_dynamic-update-slice_fusion.2
  90.9 0.7 conditional.8
  97.4 0.7 conditional.8
  101.2 2.7 %reduce.1 = bf16[512,1024]{0,1:T(8,128)(2,1)S(1)} reduce(bf16[512,1,1024]{0,2,1:T(8,128)(2,1)} %bitcast.79, bf16[]{:T(256)} %broadcast.33), dimensions={1}, to_apply=%copy.59.reduce_sub_computation | reduce | bytes 2097154 | tf_op jit(solution)/shard_map/reshape | solution.py:155
  104.5 0.8 reshape.80
  105.3 27.7 %all_to_all.66 = bf16[4,2,65536]{2,1,0:T(2,128)(2,1)S(1)} all-to-all(bf16[4,2,65536]{2,1,0:T(2,128)(2,1)S(1)} %reshape.80), channel_id=1, replica_groups=mesh['dp'=8,'seq'=4] {'seq'}, dimensions={0} | all-to-all | bytes 2097152 | tf_op jit(solution)/shard_map/all_to_all | solution.py:156
  133.0 0.9 reshape.81
  135.0 1.3 copy.61
  (147 shorter events, 32.7 us)
Async XLA Ops:
  1.7 10.9 %all-to-all-start.1 = ((bf16[128,4,128]{0,2,1:T(8,128)(2,1)}), bf16[128,4,128]{0,2,1:T(8,128)(2,1)S(1)}, u32[]{:S(2)}, u32[]{:S(2)}) async-start(bf16[128,4,128]{0,2,1:T(8,128)(2,1)} %bitcast.5), calls=%async_computation.1 | async-start | bytes 262144 | tf_op jit(solution)/shard_map/all_to_all | solution.py:135
  12.6 9.2 %all-to-all-start.2 = ((bf16[128,4,128]{0,2,1:T(8,128)(2,1)}), bf16[128,4,128]{0,2,1:T(8,128)(2,1)S(1)}, u32[]{:S(2)}, u32[]{:S(2)}) async-start(bf16[128,4,128]{0,2,1:T(8,128)(2,1)} %bitcast.12), calls=%async_computation.2 | async-start | bytes 262144 | tf_op jit(solution)/shard_map/all_to_all | solution.py:136
  15.9 9.4 %copy-start = (s32[32]{0:T(128)S(1)}, s32[32]{0:T(128)}, u32[]{:S(2)}) copy-start(s32[32]{0:T(128)} %param.13) | copy-start | bytes 388
  21.8 27.0 %all-to-all-start = ((bf16[128,4,1024]{2,0,1:T(8,128)(2,1)}), bf16[128,4,1024]{2,0,1:T(8,128)(2,1)S(1)}, u32[]{:S(2)}, u32[]{:S(2)}) async-start(bf16[128,4,1024]{2,0,1:T(8,128)(2,1)} %bitcast.58), calls=%async_computation | async-start | bytes 2097152 | tf_op jit(solution)/shard_map/all_to_all | solution.py:134
  25.9 23.3 %collective-permute-start = (bf16[256,1,128]{2,0,1:T(8,128)(2,1)S(1)}, bf16[256,1,128]{2,0,1:T(8,128)(2,1)S(1)}, u32[]{:S(2)}, u32[]{:S(2)}) collective-permute-start(bf16[256,1,128]{2,0,1:T(8,128)(2,1)S(1)} %bitcast.91), channel_id=1, source_target_pairs={{0,4},{4,8},{8,12},{12,16},{16,20},{20,24},{24,28},{1,5},{5,9},{9,... | collective-permute-start | bytes 196616 | tf_op jit(solution)/shard_map/ppermute | solution.py:17
  28.0 21.3 %collective-permute-start.1 = (bf16[256,1,128]{2,0,1:T(8,128)(2,1)S(1)}, bf16[256,1,128]{2,0,1:T(8,128)(2,1)S(1)}, u32[]{:S(2)}, u32[]{:S(2)}) collective-permute-start(bf16[256,1,128]{2,0,1:T(8,128)(2,1)S(1)} %bitcast.92), channel_id=1, source_target_pairs={{0,4},{4,8},{8,12},{12,16},{16,20},{20,24},{24,28},{1,5},{5,9},{9,... | collective-permute-start | bytes 196616 | tf_op jit(solution)/shard_map/ppermute | solution.py:17
where the time goes:
time: 137 us; the launch traced here: 136 us
  blocking collectives  27.7 us (20%)
  local copies, waits for them, and re-layouts  26.2 us (19%)
  waiting for transfers between devices  24.2 us (18%)
  loops' own time  20 us (15%)
  starting transfers between devices  17.1 us (12%)
  matrix products  10.9 us (8%)
  other arithmetic  10 us (7%)
    all_to_all x1, blocking collectives, body(): lax.all_to_all(mixed, 'seq', split_axis=0, concat_axis=1, tiled=True)  27.7 us
    another operation x1, loops' own time, attend(): per_head = lax.map(one_head, jnp.arange(heads_query, dtype=jnp.int32))  19.6 us
    all_to_all x1, waiting for transfers between devices, body(): lax.all_to_all(query_split, 'seq', split_axis=1, concat_axis=0, tiled=True)  16.2 us
    unnamed x10, local copies, waits for them, and re-layouts  6.39 us
    dynamic_update_slice x16, local copies, waits for them, and re-layouts, attend(): per_head = lax.map(one_head, jnp.arange(heads_query, dtype=jnp.int32))  6.27 us
    ppermute x2, starting transfers between devices, from_behind(): return lax.ppermute(block, axis, route)  5.42 us
    all_to_all x1, starting transfers between devices, body(): lax.all_to_all(key_split, 'seq', split_axis=1, concat_axis=0, tiled=True)  4.87 us
    dynamic_slice x8, local copies, waits for them, and re-layouts, attend(): per_head = lax.map(one_head, jnp.arange(heads_query, dtype=jnp.int32))  4.64 us
  transfers between devices with their start and end apart: 5, of which 3 were waited for; matrix products, arithmetic and copies ran while one was open for 4% of the time, Pallas kernels for 0%

commit v1 on v0

--- a/solution.py
+++ b/solution.py
@@ -153,7 +153,9 @@
         reach_rows,
     )
     mixed = mixed.reshape(block_rows, 1, local_heads * HD)
-    returned = lax.all_to_all(mixed, "seq", split_axis=0, concat_axis=1, tiled=True)
+    parts = jnp.split(mixed, lax.axis_size("seq"), axis=0)
+    received = lax.all_to_all(jnp.stack(parts), "seq", 0, 0)
+    returned = jnp.concatenate(received, axis=1)
     return returned.reshape(tok_rows, QH * HD)
 
 

time: 137 us -> 132 us (0.964)
  local copies, waits for them, and re-layouts: 26.2 us -> 23 us
  other arithmetic: 10 us -> 7.45 us
    reshape x1 -> x0, other arithmetic: 2.72 us -> none  [body(): mixed = mixed.reshape(block_rows, 1, local_heads * HD)]
    unnamed x10 -> x8, local copies, waits for them, and re-layouts: 6.39 us -> 4.47 us
    reshape x2 -> x0, local copies, waits for them, and re-layouts: 1.9 us -> none  [the longest x1 1.31 us: body(): return returned.reshape(tok_rows, QH * HD)]
    another operation x9 -> x10, local copies, waits for them, and re-layouts: 1.78 us -> 3.08 us
where the time goes in v1:
time: 132 us; the launch traced here: 131 us
  blocking collectives  27.7 us (21%)
  waiting for transfers between devices  24.7 us (19%)
  local copies, waits for them, and re-layouts  23 us (17%)
  loops' own time  20 us (15%)
  starting transfers between devices  17.1 us (13%)
  matrix products  10.9 us (8%)
  other arithmetic  7.45 us (6%)
    all_to_all x1, blocking collectives, body(): received = lax.all_to_all(jnp.stack(parts), 'seq', 0, 0)  27.7 us
    another operation x1, loops' own time, attend(): per_head = lax.map(one_head, jnp.arange(heads_query, dtype=jnp.int32))  19.6 us
    all_to_all x1, waiting for transfers between devices, body(): lax.all_to_all(query_split, 'seq', split_axis=1, concat_axis=0, tiled=True)  15.5 us
    dynamic_update_slice x16, local copies, waits for them, and re-layouts, attend(): per_head = lax.map(one_head, jnp.arange(heads_query, dtype=jnp.int32))  6.27 us
    ppermute x2, starting transfers between devices, from_behind(): return lax.ppermute(block, axis, route)  5.42 us
    all_to_all x1, starting transfers between devices, body(): lax.all_to_all(key_split, 'seq', split_axis=1, concat_axis=0, tiled=True)  4.87 us
    all_to_all x1, waiting for transfers between devices, body(): lax.all_to_all(value_split, 'seq', split_axis=1, concat_axis=0, tiled=True)  4.8 us
    dynamic_slice x8, local copies, waits for them, and re-layouts, attend(): per_head = lax.map(one_head, jnp.arange(heads_query, dtype=jnp.int32))  4.64 us
  transfers between devices with their start and end apart: 5, of which 3 were waited for; matrix products, arithmetic and copies ran while one was open for 4% of the time, Pallas kernels for 0%

profile of v1, /device:TPU:4, one launch (start us, length us, event | category | flops | bytes accessed | tf_op | source)
XLA Modules:
  0.0 131.2 jit_solution(17276034941773805597)
XLA Ops:
  0.0 1.8 %copy.33 = bf16[128,512]{0,1:T(8,128)(2,1)} copy(bf16[128,512]{1,0:T(8,128)(2,1)} %param.11) | data formatting | bytes 262144 | tf_op args[1]
  1.8 4.9 %all-to-all-start.1 = ((bf16[128,4,128]{0,2,1:T(8,128)(2,1)}), bf16[128,4,128]{0,2,1:T(8,128)(2,1)S(1)}, u32[]{:S(2)}, u32[]{:S(2)}) async-start(bf16[128,4,128]{0,2,1:T(8,128)(2,1)} %bitcast.5), calls=%async_computation.1 | async-start | bytes 262144 | tf_op jit(solution)/shard_map/all_to_all | solution.py:135
  6.6 1.7 %copy.37 = bf16[128,512]{0,1:T(8,128)(2,1)} copy(bf16[128,512]{1,0:T(8,128)(2,1)} %param.12) | data formatting | bytes 262144 | tf_op args[2]
  8.3 4.4 %all-to-all-done.1 = bf16[128,4,128]{0,2,1:T(8,128)(2,1)S(1)} async-done(((bf16[128,4,128]{0,2,1:T(8,128)(2,1)}), bf16[128,4,128]{0,2,1:T(8,128)(2,1)S(1)}, u32[]{:S(2)}, u32[]{:S(2)}) %all-to-all-start.1) | async-done | bytes 131104 | tf_op jit(solution)/shard_map/all_to_all | solution.py:135
  12.7 3.3 %all-to-all-start.2 = ((bf16[128,4,128]{0,2,1:T(8,128)(2,1)}), bf16[128,4,128]{0,2,1:T(8,128)(2,1)S(1)}, u32[]{:S(2)}, u32[]{:S(2)}) async-start(bf16[128,4,128]{0,2,1:T(8,128)(2,1)} %bitcast.12), calls=%async_computation.2 | async-start | bytes 262144 | tf_op jit(solution)/shard_map/all_to_all | solution.py:136
  16.0 1.1 copy.50
  17.1 4.8 %all-to-all-done.2 = bf16[128,4,128]{0,2,1:T(8,128)(2,1)S(1)} async-done(((bf16[128,4,128]{0,2,1:T(8,128)(2,1)}), bf16[128,4,128]{0,2,1:T(8,128)(2,1)S(1)}, u32[]{:S(2)}, u32[]{:S(2)}) %all-to-all-start.2) | async-done | bytes 131104 | tf_op jit(solution)/shard_map/all_to_all | solution.py:136
  21.9 3.5 %all-to-all-start = ((bf16[128,4,1024]{2,0,1:T(8,128)(2,1)}), bf16[128,4,1024]{2,0,1:T(8,128)(2,1)S(1)}, u32[]{:S(2)}, u32[]{:S(2)}) async-start(bf16[128,4,1024]{2,0,1:T(8,128)(2,1)} %bitcast.59), calls=%async_computation | async-start | bytes 2097152 | tf_op jit(solution)/shard_map/all_to_all | solution.py:134
  26.6 1.9 %collective-permute-start = (bf16[256,1,128]{2,0,1:T(8,128)(2,1)S(1)}, bf16[256,1,128]{2,0,1:T(8,128)(2,1)S(1)}, u32[]{:S(2)}, u32[]{:S(2)}) collective-permute-start(bf16[256,1,128]{2,0,1:T(8,128)(2,1)S(1)} %bitcast.95), channel_id=1, source_target_pairs={{0,4},{4,8},{8,12},{12,16},{16,20},{20,24},{24,28},{1,5},{5,9},{9,... | collective-permute-start | bytes 196616 | tf_op jit(solution)/shard_map/ppermute | solution.py:17
  28.7 3.5 %collective-permute-start.1 = (bf16[256,1,128]{2,0,1:T(8,128)(2,1)S(1)}, bf16[256,1,128]{2,0,1:T(8,128)(2,1)S(1)}, u32[]{:S(2)}, u32[]{:S(2)}) collective-permute-start(bf16[256,1,128]{2,0,1:T(8,128)(2,1)S(1)} %bitcast.96), channel_id=1, source_target_pairs={{0,4},{4,8},{8,12},{12,16},{16,20},{20,24},{24,28},{1,5},{5,9},{9,... | collective-permute-start | bytes 196616 | tf_op jit(solution)/shard_map/ppermute | solution.py:17
  32.2 0.9 compare_reduce_fusion
  33.4 15.5 %all-to-all-done = bf16[128,4,1024]{2,0,1:T(8,128)(2,1)S(1)} async-done(((bf16[128,4,1024]{2,0,1:T(8,128)(2,1)}), bf16[128,4,1024]{2,0,1:T(8,128)(2,1)S(1)}, u32[]{:S(2)}, u32[]{:S(2)}) %all-to-all-start) | async-done | bytes 1048608 | tf_op jit(solution)/shard_map/all_to_all | solution.py:134
  49.3 51.4 %while.12 = (s32[]{:T(128)}, bf16[8,512,128]{1,2,0:T(8,128)(2,1)}, s32[8]{0:T(128)S(1)}, bf16[512,8,128]{2,0,1:T(8,128)(2,1)S(1)}, bf16[512,1,128]{2,0,1:T(8,128...) while((s32[]{:T(128)}, bf16[8,512,128]{1,2,0:T(8,128)(2,1)}, ...), condition=%wide.region_12.13_spmd.clone.clone, body=%wide.region_3.12_spmd.clone.clone.sunk | while | flops 207420416 | bytes 8435984 | solution.py:111
  52.5 0.7 conditional.8
  55.1 0.7 constant_dynamic-update-slice_fusion.2
  58.9 0.7 conditional.8
  61.5 0.7 constant_dynamic-update-slice_fusion.2
  65.3 0.7 conditional.8
  67.9 0.7 constant_dynamic-update-slice_fusion.2
  71.8 0.7 conditional.8
  74.4 0.7 constant_dynamic-update-slice_fusion.2
  78.2 0.7 conditional.8
  80.8 0.7 constant_dynamic-update-slice_fusion.2
  84.6 0.7 conditional.8
  87.2 0.7 constant_dynamic-update-slice_fusion.2
  91.0 0.7 conditional.8
  93.6 0.7 constant_dynamic-update-slice_fusion.2
  97.5 0.7 conditional.8
  100.1 0.7 constant_dynamic-update-slice_fusion.2
  100.7 1.3 fusion.27
  102.2 27.7 %all_to_all.56 = bf16[4,128,1,1024]{1,3,2,0:T(8,128)(2,1)S(1)} all-to-all(bf16[4,128,1,1024]{1,3,2,0:T(8,128)(2,1)S(1)} %pad_maximum_fusion), channel_id=1, replica_groups=mesh['dp'=8,'seq'=4] {'seq'}, dimensions={0} | all-to-all | bytes 2097152 | tf_op jit(solution)/shard_map/all_to_all | solution.py:157
  129.9 1.3 copy.42
  (144 shorter events, 30.0 us)
Async XLA Ops:
  0.0 16.0 %copy-start = (bf16[128,4096]{1,0:T(8,128)(2,1)S(1)}, bf16[128,4096]{1,0:T(8,128)(2,1)}, u32[]{:S(2)}) copy-start(bf16[128,4096]{1,0:T(8,128)(2,1)} %param.10) | copy-start | bytes 3145732
  1.8 10.9 %all-to-all-start.1 = ((bf16[128,4,128]{0,2,1:T(8,128)(2,1)}), bf16[128,4,128]{0,2,1:T(8,128)(2,1)S(1)}, u32[]{:S(2)}, u32[]{:S(2)}) async-start(bf16[128,4,128]{0,2,1:T(8,128)(2,1)} %bitcast.5), calls=%async_computation.1 | async-start | bytes 262144 | tf_op jit(solution)/shard_map/all_to_all | solution.py:135
  12.7 9.2 %all-to-all-start.2 = ((bf16[128,4,128]{0,2,1:T(8,128)(2,1)}), bf16[128,4,128]{0,2,1:T(8,128)(2,1)S(1)}, u32[]{:S(2)}, u32[]{:S(2)}) async-start(bf16[128,4,128]{0,2,1:T(8,128)(2,1)} %bitcast.12), calls=%async_computation.2 | async-start | bytes 262144 | tf_op jit(solution)/shard_map/all_to_all | solution.py:136
  21.9 27.0 %all-to-all-start = ((bf16[128,4,1024]{2,0,1:T(8,128)(2,1)}), bf16[128,4,1024]{2,0,1:T(8,128)(2,1)S(1)}, u32[]{:S(2)}, u32[]{:S(2)}) async-start(bf16[128,4,1024]{2,0,1:T(8,128)(2,1)} %bitcast.59), calls=%async_computation | async-start | bytes 2097152 | tf_op jit(solution)/shard_map/all_to_all | solution.py:134
  25.5 0.7 copy-start.1
  26.6 22.7 %collective-permute-start = (bf16[256,1,128]{2,0,1:T(8,128)(2,1)S(1)}, bf16[256,1,128]{2,0,1:T(8,128)(2,1)S(1)}, u32[]{:S(2)}, u32[]{:S(2)}) collective-permute-start(bf16[256,1,128]{2,0,1:T(8,128)(2,1)S(1)} %bitcast.95), channel_id=1, source_target_pairs={{0,4},{4,8},{8,12},{12,16},{16,20},{20,24},{24,28},{1,5},{5,9},{9,... | collective-permute-start | bytes 196616 | tf_op jit(solution)/shard_map/ppermute | solution.py:17
  28.7 20.6 %collective-permute-start.1 = (bf16[256,1,128]{2,0,1:T(8,128)(2,1)S(1)}, bf16[256,1,128]{2,0,1:T(8,128)(2,1)S(1)}, u32[]{:S(2)}, u32[]{:S(2)}) collective-permute-start(bf16[256,1,128]{2,0,1:T(8,128)(2,1)S(1)} %bitcast.96), channel_id=1, source_target_pairs={{0,4},{4,8},{8,12},{12,16},{16,20},{20,24},{24,28},{1,5},{5,9},{9,... | collective-permute-start | bytes 196616 | tf_op jit(solution)/shard_map/ppermute | solution.py:17
